TPU v7x, 256 devices: a whole 4x4x8 slice. The times are simulated.
256 devices in a mesh: seq: 64 (over y, z, core), tp: 4 (over x).
Axes of the slice: x: 4, y: 4, z: 8, core: 2. Of those that a mesh axis runs over, the one named last changes fastest.
Arguments:
- queries_short: bfloat16 [128, 4, 2304], P('seq', None, 'tp'), may hold values from -4 to 4
- cache_short: bfloat16 [2, 128, 1024, 2304], P(None, 'seq', None, 'tp'), may hold values from -260 to 260
- fresh_short: bfloat16 [2, 128, 4, 2304], P(None, 'seq', None, 'tp'), may hold values from -260 to 260
- short_len: int32 [128], P('seq'), may hold values from 1 to 1024, as said below
- queries_long: bfloat16 [4, 4, 2304], P(None, None, 'tp'), may hold values from -4 to 4
- cache_long: bfloat16 [2, 4, 16384, 2304], P(None, None, 'seq', 'tp'), may hold values from -260 to 260
- fresh_long: bfloat16 [2, 4, 4, 2304], P(None, None, None, 'tp'), may hold values from -260 to 260
- long_len: int32 [4], replicated, may hold values from 8192 to 16384, as said below
- block_live: int32 [4, 128], P(None, 'seq'), may hold values 0 or 1
- out_weight: bfloat16 [2304, 2304], P('tp'), may hold values from -0.125 to 0.125
Outputs:
- short_out: bfloat16 [128, 4, 2304], P('seq', None, 'tp')
- long_out: bfloat16 [4, 4, 2304], P(None, None, 'tp')
Inputs may be any that keep to these rules, and one draw needn't show every extreme that they name: `short_len`: some short request fills all 1024 slots. `long_len`: some long request fills all 16384 slots.
All inputs are finite; a program needn't handle non-finite values. No bound on the sum of `block_live` on one device may be relied on, other than what follows from the above.
Results may differ from a plain program's by a relative error of at most 0.011.
Values sent between devices are 32-bit elements; how exact they have to be, the bound alone decides.
A program may use at most 64 MiB of HBM per device.

v0:
```python
import math
import jax
import jax.numpy as jnp
from jax import lax
from jax.sharding import PartitionSpec as P

HEAD_DIM = 64
NEGATIVE = -1e30


def split_heads(tensor):
    return tensor.reshape(tensor.shape[0], tensor.shape[1], tensor.shape[2] // HEAD_DIM, HEAD_DIM)


def partial_softmax(query_heads, key_heads, value_heads, usable):
    scores = jnp.einsum(
        "rjhd,rphd->rhjp", query_heads, key_heads, preferred_element_type=jnp.float32
    ) * (1.0 / math.sqrt(HEAD_DIM))
    scores = jnp.where(usable, scores, NEGATIVE)
    highest = jnp.max(scores, axis=-1)
    expo = jnp.where(usable, jnp.exp(scores - highest[..., None]), 0.0)
    totals = jnp.sum(expo, axis=-1)
    summed = jnp.einsum(
        "rhjp,rphd->rhjd",
        expo.astype(jnp.bfloat16),
        value_heads,
        preferred_element_type=jnp.float32,
    )
    return (highest, totals, summed)


def combine_parts(first, second):
    highest = jnp.maximum(first[0], second[0])
    scale_first = jnp.exp(first[0] - highest)
    scale_second = jnp.exp(second[0] - highest)
    totals = first[1] * scale_first + second[1] * scale_second
    summed = first[2] * scale_first[..., None] + second[2] * scale_second[..., None]
    return (highest, totals, summed)


def finish(parts):
    normed = (parts[2] / parts[1][..., None]).astype(jnp.bfloat16)
    normed = jnp.transpose(normed, (0, 2, 1, 3))
    return normed.reshape(normed.shape[0], normed.shape[1], normed.shape[2] * normed.shape[3])


def fresh_part(queries, fresh):
    count = queries.shape[1]
    causal = (jnp.arange(count)[:, None] >= jnp.arange(count)[None, :])[None, None]
    return partial_softmax(
        split_heads(queries), split_heads(fresh[0]), split_heads(fresh[1]), causal
    )


def per_device(
    queries_short,
    cache_short,
    fresh_short,
    short_len,
    queries_long,
    cache_long,
    fresh_long,
    long_len,
    block_live,
    out_weight,
):
    short_query = split_heads(queries_short)
    request_count = queries_short.shape[0]
    token_count = queries_short.shape[1]
    positions = cache_short.shape[2]
    usable = (jnp.arange(positions, dtype=jnp.int32)[None, :] < short_len[:, None])[
        :, None, None, :
    ]
    short_parts = partial_softmax(
        short_query, split_heads(cache_short[0]), split_heads(cache_short[1]), usable
    )
    short_att = finish(combine_parts(short_parts, fresh_part(queries_short, fresh_short)))
    local_len = cache_long.shape[2]
    spots = lax.axis_index("seq") * local_len + jnp.arange(local_len, dtype=jnp.int32)
    live = jnp.repeat(block_live, local_len // block_live.shape[1], axis=1) == 1
    long_usable = ((spots[None, :] < long_len[:, None]) & live)[:, None, None, :]
    long_parts = partial_softmax(
        split_heads(queries_long),
        split_heads(cache_long[0]),
        split_heads(cache_long[1]),
        long_usable,
    )
    every_high, every_total, every_sum = (
        lax.all_gather(long_parts[0][None], "seq", axis=0, tiled=True),
        lax.all_gather(long_parts[1][None], "seq", axis=0, tiled=True),
        lax.all_gather(long_parts[2][None], "seq", axis=0, tiled=True),
    )
    highest = jnp.max(every_high, axis=0)
    scales = jnp.exp(every_high - highest[None])
    merged = (
        highest,
        jnp.sum(every_total * scales, axis=0),
        jnp.sum(every_sum * scales[..., None], axis=0),
    )
    long_att = finish(combine_parts(merged, fresh_part(queries_long, fresh_long)))
    short_term = jnp.dot(
        short_att.reshape(-1, short_att.shape[2]), out_weight, preferred_element_type=jnp.float32
    )
    long_term = jnp.dot(
        long_att.reshape(-1, long_att.shape[2]), out_weight, preferred_element_type=jnp.float32
    )
    short_cols = lax.psum_scatter(short_term, "tp", scatter_dimension=1, tiled=True)
    long_cols = lax.psum_scatter(long_term, "tp", scatter_dimension=1, tiled=True)
    short_out = short_cols.astype(jnp.bfloat16).reshape(
        request_count, token_count, short_cols.shape[1]
    )
    long_out = long_cols.astype(jnp.bfloat16).reshape(
        long_att.shape[0], long_att.shape[1], long_cols.shape[1]
    )
    return (short_out, long_out)


def solution(mesh):
    in_specs = (
        P("seq", None, "tp"),
        P(None, "seq", None, "tp"),
        P(None, "seq", None, "tp"),
        P("seq"),
        P(None, None, "tp"),
        P(None, None, "seq", "tp"),
        P(None, None, None, "tp"),
        P(),
        P(None, "seq"),
        P("tp", None),
    )
    out_specs = (P("seq", None, "tp"), P(None, None, "tp"))
    return jax.shard_map(
        per_device, mesh=mesh, in_specs=in_specs, out_specs=out_specs, check_vma=False
    )
```

profile of v0, /device:TPU:8, one launch (start us, length us, event | category | flops | bytes accessed | tf_op | source)
XLA Modules:
  0.0 182.1 jit_solution(8602789161538166098)
XLA Ops:
  8.0 0.0 copy-start
  8.0 0.0 all-gather.5.cloned.1.call-start
  8.1 0.8 broadcast_compare_fusion
  8.9 3.2 %fusion.53 = (bf16[1,4,256,576]{2,3,1,0:T(8,128)(2,1)}, bf16[1,4,256,576]{2,3,1,0:T(8,128)(2,1)}) fusion(bf16[2,4,256,576]{2,3,1,0:T(8,128)(2,1)} %param.15), kind=kLoop, calls=%fused_computation.77 | loop fusion | bytes 4718592 | tf_op jit(solution)/shard_map/slice | solution.py:84
  12.1 0.0 copy-start.6
  12.2 0.1 reshape.139
  12.3 0.1 bitcast_and_fusion
  12.3 1.6 fusion.57
  14.0 2.4 %fusion.19 = f32[4,9,4,64]{3,2,1,0:T(4,128)} fusion(bf16[4,256,9,64]{1,3,2,0:T(8,128)(2,1)} %bitcast.96, f32[4,9,4,256]{3,2,1,0:T(4,128)S(1)} %get-tuple-element.23, f32[4,9,4]{2,1,0:T(8,128)S(1)} %get-tuple-element.22, pred[4,256]{1,0:T(4,128)(4,1)S(1)} %bitcast_and_fusion), kind=kOutput, calls=%fused_computation.30 | convolution fusion | flops 4829184 | bytes 1365568 | tf_op jit(solution)/shard_map/rhjp,rphd->rhjd/dot_general | solution.py:23
  16.3 0.0 all-gather.5.cloned.1.call-update
  16.4 0.0 reduce-scatter.7.cloned.1.call-start
  16.4 0.1 reshape.137
  16.5 0.1 reshape_squeeze.26
  16.6 0.1 fusion.29
  16.8 0.1 copy.143
  16.9 0.1 fusion.36
  17.0 0.1 copy.144
  17.1 0.1 fusion.45
  17.2 0.1 copy.147
  17.3 0.1 copy.145
  17.5 0.1 reshape_squeeze.27
  17.6 0.1 iota_compare_fusion
  17.6 2.9 %fusion.52 = (bf16[1,2,1024,576]{2,3,1,0:T(8,128)(2,1)S(1)}, bf16[1,2,1024,576]{2,3,1,0:T(8,128)(2,1)S(1)}) fusion(bf16[2,2,1024,576]{2,3,1,0:T(8,128)(2,1)} %param.11), kind=kLoop, calls=%fused_computation.76 | loop fusion | bytes 9437184 | tf_op jit(solution)/shard_map/slice | solution.py:75
  20.5 0.5 fusion.56
  21.0 0.3 fusion.11
  21.3 0.7 fusion.9
  22.1 0.2 fusion.10
  22.3 0.1 reshape_reshape.6
  22.4 2.2 %convolution_bitcast_fusion.1 = f32[2304,8]{1,0:T(8,128)} fusion(bf16[8,576]{1,0:T(8,128)(2,1)S(1)} %reshape_reshape.6, bf16[576,2304]{1,0:T(8,128)(2,1)S(1)} %copy-done), kind=kOutput, calls=%fused_computation.2 | convolution fusion | flops 21233664 | bytes 2737152
  24.6 0.0 reduce-scatter.7.cloned.1.call-update
  24.6 0.0 reduce-scatter.9.cloned.1.call-start
  24.7 0.1 copy.150
  24.8 0.2 fusion.17
  25.0 53.0 %all-gather.1 = f32[256,9,4]{1,2,0:T(4,128)S(1)} all-gather(f32[4,9,4]{1,2,0:T(4,128)S(1)} %copy.150), channel_id=3, replica_groups=mesh['seq'=64,'tp'=4] {'seq'}, dimensions={0}, use_global_device_ids=true | all-gather | bytes 37440 | tf_op jit(solution)/shard_map/all_gather | solution.py:89
  78.0 0.8 copy-done.1
  78.8 0.1 reduce_max.58
  79.0 1.2 subtract_exponential_fusion
  80.2 0.0 copy-start.2
  80.2 0.1 copy.162
  80.3 52.9 %all-gather.2 = f32[256,9,4]{1,2,0:T(4,128)} all-gather(f32[4,9,4]{1,2,0:T(4,128)S(1)} %copy.162), channel_id=4, replica_groups=mesh['seq'=64,'tp'=4] {'seq'}, dimensions={0}, use_global_device_ids=true | all-gather | bytes 37440 | tf_op jit(solution)/shard_map/all_gather | solution.py:90
  133.2 3.0 %copy.151 = f32[64,4,9,4]{3,2,1,0:T(8,128)} copy(f32[64,4,9,4]{2,3,1,0:T(4,128)S(1)} %subtract_exponential_fusion) | data formatting | bytes 73728 | tf_op jit(solution)/shard_map/exp | solution.py:94
  136.2 1.2 multiply_reduce_fusion.1
  137.5 0.1 reshape_squeeze.30
  137.6 0.2 fusion.25
  137.7 0.2 copy.154
  137.9 0.1 fusion.27
  138.1 0.1 fusion.37
  138.2 0.1 copy.157
  138.3 0.1 copy.161
  138.4 0.1 copy.165
  138.5 0.2 copy.159
  138.8 0.1 reshape_squeeze.31
  138.9 0.0 all-gather.5.cloned.1.call-done
  138.9 6.3 %multiply_reduce_fusion = f32[4,9,4,64]{3,2,1,0:T(4,128)S(1)} fusion(f32[64,4,9,4,64]{4,3,2,1,0:T(4,128)} %bitcast.91, f32[64,4,9,4]{3,2,1,0:T(8,128)} %copy.151), kind=kLoop, calls=%fused_computation | loop fusion | flops 1170432 | bytes 2433024 | tf_op jit(solution)/shard_map/reduce_sum | solution.py:98
  145.2 0.2 fusion.5
  145.4 0.1 reshape_reshape.7
  145.5 2.2 %convolution_bitcast_fusion = f32[2304,16]{1,0:T(8,128)} fusion(bf16[16,576]{1,0:T(8,128)(2,1)S(1)} %reshape_reshape.7, bf16[576,2304]{1,0:T(8,128)(2,1)S(1)} %copy-done), kind=kOutput, calls=%fused_computation.1 | convolution fusion | flops 42467328 | bytes 2820096
  147.7 0.0 reduce-scatter.9.cloned.1.call-update
  147.7 0.0 reduce-scatter.7.cloned.1.call-done
  147.7 1.0 copy.168
  148.8 0.6 reshape.138
  149.4 23.5 %reduce-scatter.9.cloned.1.call-done = f32[576,16]{1,0:T(8,128)} async-done(((f32[2304,16]{1,0:T(8,128)}), f32[576,16]{1,0:T(8,128)}) %reduce-scatter.9.cloned.1.call-update) | async-done | bytes 36880
  172.9 1.1 copy.170
  174.0 0.6 reshape.140
  (20 shorter events, 0.1 us)
Async XLA Ops:
  8.0 14.4 %copy-start = (bf16[576,2304]{1,0:T(8,128)(2,1)S(1)}, bf16[576,2304]{1,0:T(8,128)(2,1)}, u32[]{:S(2)}) copy-start(bf16[576,2304]{1,0:T(8,128)(2,1)} %param.19) | copy-start | bytes 7962628
  8.0 130.9 %all-gather.5.cloned.1.call-start = ((), (), s32[]{:S(2)}) async-start(), calls=%async_computation.2 | async-start | bytes 4792320 | tf_op jit(solution)/shard_map/all_gather | solution.py:91
  8.9 3.2 %copy-start.4 = (bf16[4,4,576]{2,1,0:T(4,128)(2,1)S(1)}, bf16[4,4,576]{2,1,0:T(4,128)(2,1)}, u32[]{:S(2)}) copy-start(bf16[4,4,576]{2,1,0:T(4,128)(2,1)} %param.14) | copy-start | bytes 55300
  8.9 3.4 %copy-start.7 = (s32[4]{0:T(128)S(1)}, s32[4]{0:T(128)}, u32[]{:S(2)}) copy-start(s32[4]{0:T(128)} %param.17) | copy-start | bytes 52
  12.1 4.3 %copy-start.5 = (bf16[2,4,576]{2,1,0:T(4,128)(2,1)S(1)}, bf16[2,4,576]{2,1,0:T(4,128)(2,1)}, u32[]{:S(2)}) copy-start(bf16[2,4,576]{2,1,0:T(4,128)(2,1)} %param.10) | copy-start | bytes 27652
  12.1 4.4 %copy-start.3 = (bf16[2,2,4,576]{3,2,1,0:T(4,128)(2,1)S(1)}, bf16[2,2,4,576]{3,2,1,0:T(4,128)(2,1)}, u32[]{:S(2)}) copy-start(bf16[2,2,4,576]{3,2,1,0:T(4,128)(2,1)} %param.12) | copy-start | bytes 55300
  12.1 5.4 %copy-start.6 = (s32[2]{0:T(128)S(1)}, s32[2]{0:T(128)}, u32[]{:S(2)}) copy-start(s32[2]{0:T(128)} %param.13) | copy-start | bytes 28
  16.4 131.4 %reduce-scatter.7.cloned.1.call-start = ((), (), s32[]{:S(2)}) async-start(), calls=%async_computation.3 | async-start | bytes 1474560
  24.6 148.3 %reduce-scatter.9.cloned.1.call-start = ((), (), s32[]{:S(2)}) async-start(), calls=%async_computation.4 | async-start | bytes 1474560
  78.0 0.8 copy-start.1
  80.2 57.3 %copy-start.2 = (bf16[2,4,4,576]{3,2,1,0:T(4,128)(2,1)S(1)}, bf16[2,4,4,576]{3,2,1,0:T(4,128)(2,1)}, u32[]{:S(2)}) copy-start(bf16[2,4,4,576]{3,2,1,0:T(4,128)(2,1)} %param.16) | copy-start | bytes 110596
Sparse Core Ops, SparseCore 0:
  16.5 81.3 all-gather.4
Sparse Core Ops, SparseCore 1:
  24.7 29.4 reduce-scatter.6
  147.8 25.1 reduce-scatter.8
where the time goes:
time: 183 us; the launch traced here: 182 us
  blocking collectives  106 us (58%)
  waiting for transfers between devices  23.6 us (13%)
  local copies, waits for them, and re-layouts  15.7 us (9%)
  between operations  15.7 us (9%)
  other arithmetic  10.8 us (6%)
  matrix products  10.3 us (6%)
    all_gather x1, blocking collectives, per_device(): lax.all_gather(long_parts[0][None], 'seq', axis=0, tiled=True)  53 us
    all_gather x1, blocking collectives, per_device(): lax.all_gather(long_parts[1][None], 'seq', axis=0, tiled=True)  52.9 us
    unnamed x5, waiting for transfers between devices  23.6 us
    reduce_sum x1, other arithmetic, per_device(): jnp.sum(every_sum * scales[..., None], axis=0)  6.27 us
    unnamed x2, matrix products  4.36 us
  transfers between devices with their start and end apart: 3, of which 1 were waited for; matrix products, arithmetic and copies ran while one was open for 14% of the time, Pallas kernels for 0%

commit v1 on v0

--- a/solution.py
+++ b/solution.py
@@ -87,7 +87,10 @@
     )
     every_high, every_total, every_sum = (
         lax.all_gather(long_parts[0][None], "seq", axis=0, tiled=True),
-        lax.all_gather(long_parts[1][None], "seq", axis=0, tiled=True),
+        jnp.concatenate(
+            lax.all_to_all(jnp.stack([long_parts[1][None]] * lax.axis_size("seq")), "seq", 0, 0),
+            axis=0,
+        ),
         lax.all_gather(long_parts[2][None], "seq", axis=0, tiled=True),
     )
     highest = jnp.max(every_high, axis=0)

time: 183 us -> 144 us (0.79)
  blocking collectives: 106 us -> 50.1 us
  starting transfers between devices: 0.13 us -> 12.2 us
  local copies, waits for them, and re-layouts: 15.7 us -> 19.1 us
    all_gather x1 -> x0, blocking collectives: 52.9 us -> none  [per_device(): lax.all_gather(long_parts[1][None], 'seq', axis=0, tiled=True)]
    all_to_all x0 -> x1, starting transfers between devices: none -> 12.1 us  [per_device(): lax.all_to_all(jnp.stack([long_parts[1][None]] * lax.axis_size('seq')), '...]
    all_gather x1, blocking collectives: 53 us -> 50.1 us  [per_device(): lax.all_gather(long_parts[0][None], 'seq', axis=0, tiled=True)]
    unnamed x18 -> x21, local copies, waits for them, and re-layouts: 2.96 us -> 5.79 us
  transfers between devices with their start and end apart: 3 -> 4, of which waited for: 1 -> 1; matrix products, arithmetic and copies ran while one was open for 14% -> 21% of each run, Pallas kernels for 0% -> 0%
where the time goes in v1:
time: 144 us; the launch traced here: 143 us
  blocking collectives  50.1 us (35%)
  waiting for transfers between devices  24.4 us (17%)
  local copies, waits for them, and re-layouts  19.1 us (13%)
  between operations  15.7 us (11%)
  starting transfers between devices  12.2 us (8%)
  other arithmetic  11.6 us (8%)
  matrix products  10.3 us (7%)
    all_gather x1, blocking collectives, per_device(): lax.all_gather(long_parts[0][None], 'seq', axis=0, tiled=True)  50.1 us
    unnamed x5, waiting for transfers between devices  24.4 us
    all_to_all x1, starting transfers between devices, per_device(): lax.all_to_all(jnp.stack([long_parts[1][None]] * lax.axis_size('seq')), '...  12.1 us
    reduce_sum x1, other arithmetic, per_device(): jnp.sum(every_sum * scales[..., None], axis=0)  6.27 us
    unnamed x21, local copies, waits for them, and re-layouts  5.79 us
    unnamed x2, matrix products  4.36 us
    dot_general x4, matrix products, partial_softmax(): jnp.einsum('rhjp,rphd->rhjd', expo.astype(jnp.bfloat16), value_heads, pre...  3.52 us
    slice x1, local copies, waits for them, and re-layouts, per_device(): cache_long[0]  3.22 us
  transfers between devices with their start and end apart: 4, of which 1 were waited for; matrix products, arithmetic and copies ran while one was open for 21% of the time, Pallas kernels for 0%

profile of v1, /device:TPU:8, one launch (start us, length us, event | category | flops | bytes accessed | tf_op | source)
XLA Modules:
  0.0 143.3 jit_solution(17467548271861947453)
XLA Ops:
  8.0 0.0 all-gather.4.cloned.1.call-start
  8.1 0.8 broadcast_compare_fusion
  8.9 3.2 %fusion.54 = (bf16[1,4,256,576]{2,3,1,0:T(8,128)(2,1)}, bf16[1,4,256,576]{2,3,1,0:T(8,128)(2,1)}) fusion(bf16[2,4,256,576]{2,3,1,0:T(8,128)(2,1)} %param.15), kind=kLoop, calls=%fused_computation.78 | loop fusion | bytes 4718592 | tf_op jit(solution)/shard_map/slice | solution.py:84
  12.1 0.1 reshape.144
  12.3 0.1 bitcast_and_fusion
  12.3 1.6 %fusion.58 = (f32[4,9,4]{2,1,0:T(8,128)S(1)}, f32[4,9,4,256]{3,2,1,0:T(4,128)S(1)}) fusion(bf16[4,256,9,64]{1,3,2,0:T(8,128)(2,1)} %bitcast.100, bf16[4,4,9,64]{3,2,1,0:T(8,128)(2,1)S(1)} %reshape.144, pred[4,256]{1,0:T(4,128)(4,1)S(1)} %bitcast_and_fusion), kind=kOutput, calls=%fused_computation.82 | convolution fusion | flops 4829040 | bytes 1347136 | tf_op jit(solution)/shard_map/rjhd,rphd->rhjp/dot_general | solution.py:16
  14.0 2.4 %fusion.20 = f32[4,9,4,64]{3,2,1,0:T(4,128)} fusion(bf16[4,256,9,64]{1,3,2,0:T(8,128)(2,1)} %bitcast.102, f32[4,9,4,256]{3,2,1,0:T(4,128)S(1)} %get-tuple-element.23, f32[4,9,4]{2,1,0:T(8,128)S(1)} %get-tuple-element.22, pred[4,256]{1,0:T(4,128)(4,1)S(1)} %bitcast_and_fusion), kind=kOutput, calls=%fused_computation.31 | convolution fusion | flops 4829184 | bytes 1365568 | tf_op jit(solution)/shard_map/rhjp,rphd->rhjd/dot_general | solution.py:23
  16.4 0.2 fusion.18
  16.6 0.1 copy.162
  16.7 0.1 broadcast_bitcast_fusion
  16.8 1.3 reshape.153
  18.0 12.1 %all-to-all-start = ((f32[64,1,144]{2,1,0:T(1,128)}), f32[64,1,144]{2,1,0:T(1,128)S(1)}, u32[]{:S(2)}, u32[]{:S(2)}) async-start(f32[64,1,144]{2,1,0:T(1,128)} %reshape.153), calls=%async_computation | async-start | bytes 131072 | tf_op jit(solution)/shard_map/all_to_all | solution.py:91
  30.1 0.0 reduce-scatter.7.cloned.1.call-start
  30.2 0.1 reshape.142
  30.3 0.1 reshape_squeeze.26
  30.4 0.1 fusion.30
  30.5 0.1 copy.143
  30.7 0.1 fusion.37
  30.8 0.1 copy.144
  30.9 0.1 fusion.46
  31.0 0.1 copy.147
  31.1 0.1 copy.145
  31.2 0.1 reshape_squeeze.27
  31.3 0.1 iota_compare_fusion
  31.4 2.9 %fusion.53 = (bf16[1,2,1024,576]{2,3,1,0:T(8,128)(2,1)S(1)}, bf16[1,2,1024,576]{2,3,1,0:T(8,128)(2,1)S(1)}) fusion(bf16[2,2,1024,576]{2,3,1,0:T(8,128)(2,1)} %param.11), kind=kLoop, calls=%fused_computation.77 | loop fusion | bytes 9437184 | tf_op jit(solution)/shard_map/slice | solution.py:75
  34.4 0.5 fusion.57
  34.9 0.3 fusion.12
  35.1 0.7 fusion.9
  35.9 0.2 fusion.10
  36.1 0.1 reshape_reshape.6
  36.2 2.2 %convolution_bitcast_fusion.1 = f32[2304,8]{1,0:T(8,128)} fusion(bf16[8,576]{1,0:T(8,128)(2,1)S(1)} %reshape_reshape.6, bf16[576,2304]{1,0:T(8,128)(2,1)S(1)} %copy-done), kind=kOutput, calls=%fused_computation.2 | convolution fusion | flops 21233664 | bytes 2737152
  38.4 0.0 reduce-scatter.7.cloned.1.call-update
  38.4 0.0 reduce-scatter.9.cloned.1.call-start
  38.5 0.1 copy.150
  38.6 50.1 %all-gather.1 = f32[256,9,4]{1,2,0:T(4,128)S(1)} all-gather(f32[4,9,4]{1,2,0:T(4,128)S(1)} %copy.150), channel_id=3, replica_groups=mesh['seq'=64,'tp'=4] {'seq'}, dimensions={0}, use_global_device_ids=true | all-gather | bytes 37440 | tf_op jit(solution)/shard_map/all_gather | solution.py:89
  88.7 0.8 copy-done.1
  89.5 0.1 reduce_max.58
  89.6 1.2 subtract_exponential_fusion
  90.9 0.1 reshape_squeeze.30
  91.0 0.2 fusion.26
  91.1 0.2 copy.154
  91.3 0.1 fusion.28
  91.5 0.1 fusion.38
  91.6 3.0 %copy.151 = f32[64,4,9,4]{3,2,1,0:T(8,128)} copy(f32[64,4,9,4]{2,3,1,0:T(4,128)S(1)} %subtract_exponential_fusion) | data formatting | bytes 73728 | tf_op jit(solution)/shard_map/exp | solution.py:97
  94.6 0.2 copy.159
  94.8 0.1 reshape_squeeze.31
  94.9 0.5 broadcast.55
  95.4 0.8 reduce
  96.2 1.5 %reshape.154 = f32[64,1,4,4,9]{4,3,2,1,0:T(4,128)} reshape(f32[64,144]{1,0:T(8,128)S(1)} %reduce) | data formatting | bytes 73728
  97.8 1.2 fusion.11
  99.0 0.1 copy.157
  99.1 0.1 copy.161
  99.2 0.1 copy.165
  99.4 6.3 %multiply_reduce_fusion = f32[4,9,4,64]{3,2,1,0:T(4,128)S(1)} fusion(f32[64,4,9,4,64]{4,3,2,1,0:T(4,128)} %bitcast.98, f32[64,4,9,4]{3,2,1,0:T(8,128)} %copy.151), kind=kLoop, calls=%fused_computation | loop fusion | flops 1170432 | bytes 2433024 | tf_op jit(solution)/shard_map/reduce_sum | solution.py:101
  105.6 0.2 fusion.5
  105.9 0.1 reshape_reshape.7
  106.0 2.2 %convolution_bitcast_fusion = f32[2304,16]{1,0:T(8,128)} fusion(bf16[16,576]{1,0:T(8,128)(2,1)S(1)} %reshape_reshape.7, bf16[576,2304]{1,0:T(8,128)(2,1)S(1)} %copy-done), kind=kOutput, calls=%fused_computation.1 | convolution fusion | flops 42467328 | bytes 2820096
  108.2 0.0 reduce-scatter.9.cloned.1.call-update
  108.2 0.0 reduce-scatter.7.cloned.1.call-done
  108.2 1.0 copy.168
  109.3 0.6 reshape.143
  109.9 24.3 %reduce-scatter.9.cloned.1.call-done = f32[576,16]{1,0:T(8,128)} async-done(((f32[2304,16]{1,0:T(8,128)}), f32[576,16]{1,0:T(8,128)}) %reduce-scatter.9.cloned.1.call-update) | async-done | bytes 36880
  134.2 1.1 copy.170
  135.3 0.6 reshape.146
  (26 shorter events, 0.2 us)
Async XLA Ops:
  8.0 28.2 %copy-start = (bf16[576,2304]{1,0:T(8,128)(2,1)S(1)}, bf16[576,2304]{1,0:T(8,128)(2,1)}, u32[]{:S(2)}) copy-start(bf16[576,2304]{1,0:T(8,128)(2,1)} %param.19) | copy-start | bytes 7962628
  8.0 91.3 %all-gather.4.cloned.1.call-start = ((), (), s32[]{:S(2)}) async-start(), calls=%async_computation.3 | async-start | bytes 4792320 | tf_op jit(solution)/shard_map/all_gather | solution.py:94
  8.9 3.2 %copy-start.4 = (bf16[4,4,576]{2,1,0:T(4,128)(2,1)S(1)}, bf16[4,4,576]{2,1,0:T(4,128)(2,1)}, u32[]{:S(2)}) copy-start(bf16[4,4,576]{2,1,0:T(4,128)(2,1)} %param.14) | copy-start | bytes 55300
  8.9 3.3 %copy-start.7 = (s32[4]{0:T(128)S(1)}, s32[4]{0:T(128)}, u32[]{:S(2)}) copy-start(s32[4]{0:T(128)} %param.17) | copy-start | bytes 52
  12.1 18.1 %copy-start.5 = (bf16[2,4,576]{2,1,0:T(4,128)(2,1)S(1)}, bf16[2,4,576]{2,1,0:T(4,128)(2,1)}, u32[]{:S(2)}) copy-start(bf16[2,4,576]{2,1,0:T(4,128)(2,1)} %param.10) | copy-start | bytes 27652
  12.1 18.1 %copy-start.3 = (bf16[2,2,4,576]{3,2,1,0:T(4,128)(2,1)S(1)}, bf16[2,2,4,576]{3,2,1,0:T(4,128)(2,1)}, u32[]{:S(2)}) copy-start(bf16[2,2,4,576]{3,2,1,0:T(4,128)(2,1)} %param.12) | copy-start | bytes 55300
  12.3 19.0 %copy-start.6 = (s32[2]{0:T(128)S(1)}, s32[2]{0:T(128)}, u32[]{:S(2)}) copy-start(s32[2]{0:T(128)} %param.13) | copy-start | bytes 28
  18.0 76.9 %all-to-all-start = ((f32[64,1,144]{2,1,0:T(1,128)}), f32[64,1,144]{2,1,0:T(1,128)S(1)}, u32[]{:S(2)}, u32[]{:S(2)}) async-start(f32[64,1,144]{2,1,0:T(1,128)} %reshape.153), calls=%async_computation | async-start | bytes 131072 | tf_op jit(solution)/shard_map/all_to_all | solution.py:91
  30.1 78.1 %reduce-scatter.7.cloned.1.call-start = ((), (), s32[]{:S(2)}) async-start(), calls=%async_computation.4 | async-start | bytes 1474560
  38.4 52.4 %copy-start.2 = (bf16[2,4,4,576]{3,2,1,0:T(4,128)(2,1)S(1)}, bf16[2,4,4,576]{3,2,1,0:T(4,128)(2,1)}, u32[]{:S(2)}) copy-start(bf16[2,4,4,576]{3,2,1,0:T(4,128)(2,1)} %param.16) | copy-start | bytes 110596
  38.4 95.8 %reduce-scatter.9.cloned.1.call-start = ((), (), s32[]{:S(2)}) async-start(), calls=%async_computation.5 | async-start | bytes 1474560
  88.7 0.8 copy-start.1
Sparse Core Ops, SparseCore 0:
  16.5 81.0 all-gather.3
Sparse Core Ops, SparseCore 1:
  38.5 27.6 reduce-scatter.6
  108.3 25.9 reduce-scatter.8
